TPU v7x, 256 devices: a whole 4x4x8 slice. The times are simulated.
256 devices in a mesh: tm: 32 (over x, z), tensor: 8 (over y, core).
Axes of the slice: x: 4, y: 4, z: 8, core: 2. Of those that a mesh axis runs over, the one named last changes fastest.
Arguments:
- latents: float32 [32, 640, 64], P('tm', 'tensor'), may hold values from -6 to 6
- residual: bfloat16 [32, 640, 5120], P('tm'), may hold values from -6 to 6
- timesteps: int32 [32], P('tm'), may hold values from 0 to 999
- step_sizes: float32 [32], P('tm'), may hold values from 0.015 to 0.06
- embed_weight: bfloat16 [64, 5120], replicated
- mod_weight: bfloat16 [3, 256, 5120], P(None, None, 'tensor'), may hold values from -0.75 to 0.75
- up_weight: bfloat16 [5120, 7168], P('tm', 'tensor'), may hold values from -0.078125 to 0.078125
- down_weight: bfloat16 [7168, 5120], P('tensor', 'tm'), may hold values from -0.0625 to 0.0625
- head_weight: bfloat16 [5120, 64], replicated, may hold values from -0.078125 to 0.078125
Outputs:
- drift: float32 [32, 640, 64], P('tm', 'tensor')
- new_latents: float32 [32, 640, 64], P('tm', 'tensor')
All inputs are finite; a program needn't handle non-finite values.
Results may differ from a plain program's by a relative error of at most 0.0085.
Values may be sent and summed in bfloat16 or wider, within the bound.
No kernel may reach another device: no remote copies, remote signals or barrier semaphores. Data moves between devices by JAX's collectives and lax.ppermute only.
A program may use at most 128 MiB of HBM per device.

v0:
```python
import math
import jax
import jax.numpy as jnp
from jax import lax
from jax.sharding import PartitionSpec as P


def prefix(part, axis, combine, identity):
    place = lax.axis_index(axis)
    gathered = lax.all_gather(part, axis)
    state = jnp.zeros_like(part) + jnp.asarray(identity, part.dtype)

    def one(hop, state):
        return combine(state, lax.dynamic_index_in_dim(gathered, hop, 0, False))

    return lax.fori_loop(0, place, one, state)


def normalize(values):
    centre = values - jnp.mean(values, axis=-1, keepdims=True)
    spread = jnp.mean(centre * centre, axis=-1, keepdims=True)
    return centre * lax.rsqrt(spread + 1e-06)


def time_features(stamps, width):
    half = width // 2
    freqs = jnp.exp(-math.log(10000.0) * jnp.arange(half, dtype=jnp.float32) / half)
    angles = stamps.astype(jnp.float32)[:, None] * freqs[None, :]
    return jnp.concatenate([jnp.cos(angles), jnp.sin(angles)], axis=-1)


def add_terms(earlier, later):
    return earlier + later


def local(
    latents,
    residual,
    timesteps,
    step_sizes,
    embed_weight,
    mod_weight,
    up_weight,
    down_weight,
    head_weight,
):
    feature = jax.nn.silu(time_features(timesteps, mod_weight.shape[1])).astype(jnp.bfloat16)[0]
    piece_mod = jnp.einsum("f,kfd->kd", feature, mod_weight, preferred_element_type=jnp.float32)
    modulation = lax.all_gather(piece_mod, "tensor", axis=1, tiled=True)
    latent = latents[0]
    stream = residual[0]
    latent_bf = latent.astype(jnp.bfloat16)
    own_rows = latent.shape[0]
    row_start = lax.axis_index("tensor") * own_rows
    own_stream = lax.dynamic_slice_in_dim(stream, row_start, own_rows, 0)
    hidden = own_stream.astype(jnp.float32) + jnp.dot(
        latent_bf, embed_weight, preferred_element_type=jnp.float32
    )
    local_normed = (normalize(hidden) * (1.0 + modulation[1]) + modulation[0]).astype(jnp.bfloat16)
    normed = lax.all_gather(local_normed, "tensor", axis=0, tiled=True)
    preact = jnp.dot(
        normed,
        lax.all_gather(up_weight, "tm", axis=0, tiled=True),
        preferred_element_type=jnp.float32,
    )
    activated = jax.nn.gelu(preact, approximate=True).astype(jnp.bfloat16)
    partial_sums = jnp.dot(
        activated,
        lax.all_gather(down_weight, "tm", axis=1, tiled=True),
        preferred_element_type=jnp.float32,
    )
    mixed = lax.psum_scatter(
        partial_sums.astype(jnp.bfloat16), "tensor", scatter_dimension=0, tiled=True
    ).astype(jnp.float32)
    updated = hidden + modulation[2] * mixed
    drift = jnp.dot(
        normalize(updated).astype(jnp.bfloat16), head_weight, preferred_element_type=jnp.float32
    )
    position = lax.axis_index("tm")
    first = (position == 0).astype(jnp.float32)
    term = first * latent - step_sizes[0] * drift
    earlier = prefix(term, "tm", add_terms, jnp.zeros_like(term))
    new_latent = earlier + term
    return (drift[None], new_latent[None])


def solution(mesh):
    in_specs = (
        P("tm", "tensor", None),
        P("tm", None, None),
        P("tm"),
        P("tm"),
        P(),
        P(None, None, "tensor"),
        P("tm", "tensor"),
        P("tensor", "tm"),
        P(),
    )
    out_specs = (P("tm", "tensor", None), P("tm", "tensor", None))
    return jax.shard_map(local, mesh=mesh, in_specs=in_specs, out_specs=out_specs, check_vma=False)
```

profile of v0, /device:TPU:6, one launch (start us, length us, event | category | flops | bytes accessed | tf_op | source)
XLA Modules:
  0.0 398.8 jit_solution(11767064728763271483)
XLA Ops:
  7.2 0.0 copy-start
  7.2 0.0 all-gather.6.cloned.1.call-start
  7.2 1.9 fusion.28
  9.2 0.3 multiply_reduce_fusion.1
  10.3 0.0 copy-done
  10.3 0.2 fusion.29
  10.5 13.3 %all_gather.18 = f32[3,5120]{1,0:T(4,128)S(1)} all-gather(f32[3,640]{1,0:T(4,128)S(1)} %bitcast.46), channel_id=1, replica_groups=mesh['tm'=32,'tensor'=8] {'tensor'}, dimensions={1}, use_global_device_ids=true | all-gather | bytes 69120 | tf_op jit(solution)/shard_map/all_gather | solution.py:49
  23.9 1.3 add_convert_fusion
  25.2 0.0 all-gather.6.cloned.1.call-update
  25.2 0.0 all-gather.8.cloned.1.call-start
  25.2 0.7 all-gather.8.cloned.1.call-update
  26.0 0.0 all-gather.10.cloned.1.call-start
  26.0 0.7 all-gather.10.cloned.1.call-update
  26.7 0.0 reduce-scatter.2.cloned.1.call-start
  26.7 45.4 %all-gather.6.cloned.1.call-done = bf16[640,5120]{1,0:T(8,128)(2,1)} async-done(((bf16[80,5120]{1,0:T(8,128)(2,1)}), bf16[640,5120]{1,0:T(8,128)(2,1)}) %all-gather.6.cloned.1.call-update) | async-done | bytes 6553616 | tf_op jit(solution)/shard_map/all_gather | solution.py:60
  72.2 103.0 %all-gather.8.cloned.1.call-done = bf16[5120,896]{1,0:T(8,128)(2,1)} async-done(((bf16[160,896]{1,0:T(8,128)(2,1)}), bf16[5120,896]{1,0:T(8,128)(2,1)}) %all-gather.8.cloned.1.call-update) | async-done | bytes 9175056 | tf_op jit(solution)/shard_map/all_gather | solution.py:63
  175.2 12.7 %fusion.30 = f32[640,896]{1,0:T(8,128)} fusion(bf16[640,5120]{1,0:T(8,128)(2,1)} %all-gather.6.cloned.1.call-done, bf16[5120,896]{1,0:T(8,128)(2,1)} %all-gather.8.cloned.1.call-done), kind=kOutput, calls=%fused_computation.50 | convolution fusion | flops 5872025600 | bytes 18022400 | tf_op jit(solution)/shard_map/dot_general | solution.py:61
  187.9 89.2 %all-gather.10.cloned.1.call-done = bf16[896,5120]{0,1:T(8,128)(2,1)} async-done(((bf16[896,160]{0,1:T(8,128)(2,1)}), bf16[896,5120]{0,1:T(8,128)(2,1)}) %all-gather.10.cloned.1.call-update) | async-done | bytes 9175056 | tf_op jit(solution)/shard_map/all_gather | solution.py:69
  277.1 12.2 %convolution_convert_fusion = bf16[640,5120]{1,0:T(8,128)(2,1)} fusion(bf16[896,5120]{0,1:T(8,128)(2,1)} %all-gather.10.cloned.1.call-done, f32[640,896]{1,0:T(8,128)} %fusion.30), kind=kOutput, calls=%fused_computation.2 | convolution fusion | flops 5880463360 | bytes 18022400 | tf_op jit(solution)/shard_map/dot_general | solution.py:67
  289.2 0.0 reduce-scatter.2.cloned.1.call-update
  289.9 44.7 %reduce-scatter.2.cloned.1.call-done = bf16[80,5120]{1,0:T(8,128)(2,1)} async-done(((bf16[640,5120]{1,0:T(8,128)(2,1)}), bf16[80,5120]{1,0:T(8,128)(2,1)}) %reduce-scatter.2.cloned.1.call-update) | async-done | bytes 819216 | tf_op jit(solution)/shard_map/reduce_scatter | solution.py:72
  334.6 0.0 copy-start.1
  334.6 1.5 fusion.16
  336.2 0.0 copy-start.2
  336.2 0.0 copy-done.1
  336.2 0.5 multiply_reduce_fusion
  336.7 0.0 copy-start.3
  336.7 0.6 copy-done.2
  337.3 0.6 fusion.13
  337.9 0.0 copy-start.4
  337.9 0.0 copy-done.3
  337.9 50.2 %all-gather.1 = f32[32,80,64]{1,2,0:T(8,128)S(1)} all-gather(f32[1,80,64]{1,2,0:T(8,128)S(1)} %fusion.19), channel_id=2, replica_groups=mesh['tm'=32,'tensor'=8] {'tm'}, dimensions={0}, use_global_device_ids=true | all-gather | bytes 675840 | tf_op jit(solution)/shard_map/all_gather | solution.py:10
  388.1 3.4 while.10
  388.2 0.1 copy.20
  388.3 0.1 copy.20
  388.4 0.1 copy.20
  388.6 0.1 copy.20
  388.7 0.1 copy.20
  388.9 0.1 copy.20
  389.0 0.1 copy.20
  389.2 0.1 copy.20
  389.3 0.1 copy.20
  389.4 0.1 copy.20
  389.6 0.1 copy.20
  389.7 0.1 copy.20
  389.9 0.1 copy.20
  390.0 0.1 copy.20
  390.1 0.1 copy.20
  390.3 0.1 copy.20
  390.4 0.1 copy.20
  390.6 0.1 copy.20
  390.7 0.1 copy.20
  390.9 0.1 copy.20
  391.0 0.1 copy.20
  391.1 0.1 copy.20
  391.3 0.1 copy.20
  391.4 0.1 copy.20
  391.5 0.1 copy.14
  391.6 0.6 add_bitcast_fusion
  392.2 0.0 copy-done.4
  (59 shorter events, 0.6 us)
Async XLA Ops:
  7.2 3.1 copy-start
  7.2 65.0 %all-gather.6.cloned.1.call-start = ((), (), s32[]{:S(2)}) async-start(), calls=%async_computation.1 | async-start | bytes 7372800 | tf_op jit(solution)/shard_map/all_gather | solution.py:60
  25.2 150.0 %all-gather.8.cloned.1.call-start = ((), (), s32[]{:S(2)}) async-start(), calls=%async_computation.2 | async-start | bytes 9461760 | tf_op jit(solution)/shard_map/all_gather | solution.py:63
  26.0 251.1 %all-gather.10.cloned.1.call-start = ((), (), s32[]{:S(2)}) async-start(), calls=%async_computation.3 | async-start | bytes 9461760 | tf_op jit(solution)/shard_map/all_gather | solution.py:69
  26.7 307.9 %reduce-scatter.2.cloned.1.call-start = ((), (), s32[]{:S(2)}) async-start(), calls=%async_computation.4 | async-start | bytes 7372800 | tf_op jit(solution)/shard_map/reduce_scatter | solution.py:72
  334.6 1.6 copy-start.1
  336.2 1.1 copy-start.2
  336.7 1.2 copy-start.3
  337.9 54.4 %copy-start.4 = (f32[80,64]{0,1:T(8,128)}, f32[80,64]{0,1:T(8,128)S(1)}, u32[]{:S(2)}) copy-start(f32[80,64]{0,1:T(8,128)S(1)} %fusion.13) | copy-start | bytes 61444
Sparse Core Ops, SparseCore 0:
  25.3 46.7 all-gather.5
  74.7 100.4 all-gather.7
  177.8 99.2 all-gather.9
  289.4 45.1 reduce-scatter.1
where the time goes:
time: 399 us
  waiting for transfers between devices  284 us (71%)
  blocking collectives  63.5 us (16%)
  matrix products  27.6 us (7%)
  between operations  15.2 us (4%)
  other arithmetic  4.66 us (1%)
    all_gather x1, waiting for transfers between devices, local(): lax.all_gather(up_weight, 'tm', axis=0, tiled=True)  103 us
    all_gather x1, waiting for transfers between devices, local(): lax.all_gather(down_weight, 'tm', axis=1, tiled=True)  89.2 us
    all_gather x1, blocking collectives, prefix(): gathered = lax.all_gather(part, axis)  50.2 us
    all_gather x1, waiting for transfers between devices, local(): normed = lax.all_gather(local_normed, 'tensor', axis=0, tiled=True)  45.4 us
    reduce_scatter x1, waiting for transfers between devices, local(): lax.psum_scatter(partial_sums.astype(jnp.bfloat16), 'tensor', scatter_dim...  44.7 us
    all_gather x1, blocking collectives, local(): modulation = lax.all_gather(piece_mod, 'tensor', axis=1, tiled=True)  13.3 us
    dot_general x1, matrix products, local(): jnp.dot(normed, lax.all_gather(up_weight, 'tm', axis=0, tiled=True), pref...  12.7 us
    dot_general x1, matrix products, local(): jnp.dot(activated, lax.all_gather(down_weight, 'tm', axis=1, tiled=True),...  12.2 us
  transfers between devices with their start and end apart: 4, of which 4 were waited for; matrix products, arithmetic and copies ran while one was open for 3% of the time, Pallas kernels for 0%

commit v1 on v0

--- a/solution.py
+++ b/solution.py
@@ -3,6 +3,22 @@
 import jax.numpy as jnp
 from jax import lax
 from jax.sharding import PartitionSpec as P
+
+
+def gather_around(x, axis, dim):
+    ways, here, step = (lax.axis_size(axis), lax.axis_index(axis), x.shape[dim])
+    lengths = [n * ways if d == dim else n for d, n in enumerate(x.shape)]
+    full = lax.dynamic_update_slice_in_dim(jnp.zeros(lengths, x.dtype), x, here * step, axis=dim)
+    going_up = going_down = x
+    for far in range(1, ways // 2 + 1):
+        going_up = lax.ppermute(going_up, axis, [(d, (d + 1) % ways) for d in range(ways)])
+        full = lax.dynamic_update_slice_in_dim(full, going_up, (here - far) % ways * step, axis=dim)
+        if 2 * far < ways:
+            going_down = lax.ppermute(going_down, axis, [(d, (d - 1) % ways) for d in range(ways)])
+            full = lax.dynamic_update_slice_in_dim(
+                full, going_down, (here + far) % ways * step, axis=dim
+            )
+    return full
 
 
 def prefix(part, axis, combine, identity):
@@ -57,7 +73,7 @@
         latent_bf, embed_weight, preferred_element_type=jnp.float32
     )
     local_normed = (normalize(hidden) * (1.0 + modulation[1]) + modulation[0]).astype(jnp.bfloat16)
-    normed = lax.all_gather(local_normed, "tensor", axis=0, tiled=True)
+    normed = gather_around(local_normed, "tensor", 0)
     preact = jnp.dot(
         normed,
         lax.all_gather(up_weight, "tm", axis=0, tiled=True),

time: 399 us -> 337 us (0.84)
  waiting for transfers between devices: 284 us -> 202 us
  local copies, waits for them, and re-layouts: 2.8 us -> 13.5 us
  starting transfers between devices: 0.16 us -> 8.99 us
    all_gather x1, waiting for transfers between devices: 103 us -> 30.2 us  [local(): lax.all_gather(up_weight, 'tm', axis=0, tiled=True)]
    all_gather x1 -> x0, waiting for transfers between devices: 45.4 us -> none  [local(): normed = lax.all_gather(local_normed, 'tensor', axis=0, tiled=True)]
    ppermute x0 -> x7, waiting for transfers between devices: none -> 36.7 us  [the longest x4 36.7 us: gather_around(): lax.ppermute(going_up, axis, [(d, (d + 1) % ways) for d in range(ways)])]
    ppermute x0 -> x7, starting transfers between devices: none -> 8.87 us  [the longest x3 8.52 us: gather_around(): lax.ppermute(going_down, axis, [(d, (d - 1) % ways) for d in range(ways)])]
    dynamic_update_slice x0 -> x7, local copies, waits for them, and re-layouts: none -> 7.84 us  [the longest x4 4.97 us: gather_around(): lax.dynamic_update_slice_in_dim(full, going_up, (here - far) % ways * ste...]
  transfers between devices with their start and end apart: 4 -> 10, of which waited for: 4 -> 7; matrix products, arithmetic and copies ran while one was open for 3% -> 8% of each run, Pallas kernels for 0% -> 0%
where the time goes in v1:
time: 337 us
  waiting for transfers between devices  202 us (60%)
  blocking collectives  63.5 us (19%)
  matrix products  27.5 us (8%)
  between operations  15.2 us (5%)
  local copies, waits for them, and re-layouts  13.5 us (4%)
  starting transfers between devices  8.99 us (3%)
  other arithmetic  4.92 us (1%)
    all_gather x1, waiting for transfers between devices, local(): lax.all_gather(down_weight, 'tm', axis=1, tiled=True)  89.2 us
    all_gather x1, blocking collectives, prefix(): gathered = lax.all_gather(part, axis)  50.2 us
    reduce_scatter x1, waiting for transfers between devices, local(): lax.psum_scatter(partial_sums.astype(jnp.bfloat16), 'tensor', scatter_dim...  44.7 us
    ppermute x4, waiting for transfers between devices, gather_around(): lax.ppermute(going_up, axis, [(d, (d + 1) % ways) for d in range(ways)])  36.7 us
    all_gather x1, waiting for transfers between devices, local(): lax.all_gather(up_weight, 'tm', axis=0, tiled=True)  30.2 us
    all_gather x1, blocking collectives, local(): modulation = lax.all_gather(piece_mod, 'tensor', axis=1, tiled=True)  13.3 us
    dot_general x1, matrix products, local(): jnp.dot(normed, lax.all_gather(up_weight, 'tm', axis=0, tiled=True), pref...  12.7 us
    dot_general x1, matrix products, local(): jnp.dot(activated, lax.all_gather(down_weight, 'tm', axis=1, tiled=True),...  12.2 us
  transfers between devices with their start and end apart: 10, of which 7 were waited for; matrix products, arithmetic and copies ran while one was open for 8% of the time, Pallas kernels for 0%

profile of v1, /device:TPU:6, one launch (start us, length us, event | category | flops | bytes accessed | tf_op | source)
XLA Modules:
  0.0 336.9 jit_solution(8423143687398635617)
XLA Ops:
  7.2 0.0 all-gather.5.cloned.1.call-start
  7.2 0.7 all-gather.5.cloned.1.call-update
  7.9 0.0 all-gather.7.cloned.1.call-start
  8.0 0.7 all-gather.7.cloned.1.call-update
  8.7 0.0 reduce-scatter.2.cloned.1.call-start
  9.5 0.2 fusion.29
  9.7 13.3 %all_gather.15 = f32[3,5120]{1,0:T(4,128)S(1)} all-gather(f32[3,640]{1,0:T(4,128)S(1)} %bitcast.46), channel_id=1, replica_groups=mesh['tm'=32,'tensor'=8] {'tensor'}, dimensions={1}, use_global_device_ids=true | all-gather | bytes 69120 | tf_op jit(solution)/shard_map/all_gather | solution.py:65
  23.0 1.9 fusion.28
  24.9 0.3 multiply_reduce_fusion.1
  25.2 0.1 fusion.27
  25.3 3.5 %broadcast_in_dim.8 = bf16[640,5120]{1,0:T(8,128)(2,1)} broadcast(bf16[]{:T(256)} %constant.89.clone.1), dimensions={} | broadcast | bytes 6553602 | tf_op jit(solution)/shard_map/broadcast_in_dim | solution.py:11
  28.8 1.5 constant_dynamic-update-slice_fusion.7
  30.3 0.3 collective-permute-start
  30.6 2.6 collective-permute-start.1
  33.3 10.3 %collective-permute-done = bf16[80,5120]{1,0:T(8,128)(2,1)} collective-permute-done((bf16[80,5120]{1,0:T(8,128)(2,1)}, bf16[80,5120]{1,0:T(8,128)(2,1)}, u32[]{:S(2)}, u32[]{:S(2)}) %collective-permute-start) | collective-permute-done | bytes 819232 | tf_op jit(solution)/shard_map/ppermute | solution.py:14
  43.6 3.0 collective-permute-start.3
  46.6 2.1 constant_dynamic-update-slice_fusion.6
  48.6 1.0 constant_dynamic-update-slice_fusion.5
  49.6 7.2 %collective-permute-done.2 = bf16[80,5120]{1,0:T(8,128)(2,1)S(1)} collective-permute-done((bf16[80,5120]{1,0:T(8,128)(2,1)}, bf16[80,5120]{1,0:T(8,128)(2,1)S(1)}, u32[]{:S(2)}, u32[]{:S(2)}) %collective-permute-start.2) | collective-permute-done | bytes 819232 | tf_op jit(solution)/shard_map/ppermute | solution.py:14
  56.8 3.0 collective-permute-start.5
  59.7 1.0 constant_dynamic-update-slice_fusion.4
  60.7 1.0 constant_dynamic-update-slice_fusion.3
  61.7 8.1 %collective-permute-done.4 = bf16[80,5120]{1,0:T(8,128)(2,1)S(1)} collective-permute-done((bf16[80,5120]{1,0:T(8,128)(2,1)S(1)}, bf16[80,5120]{1,0:T(8,128)(2,1)S(1)}, u32[]{:S(2)}, u32[]{:S(2)}) %collective-permute-start.4) | collective-permute-done | bytes 819232 | tf_op jit(solution)/shard_map/ppermute | solution.py:14
  69.8 1.0 constant_dynamic-update-slice_fusion.2
  70.7 0.9 constant_dynamic-update-slice_fusion.1
  71.7 11.1 %collective-permute-done.6 = bf16[80,5120]{1,0:T(8,128)(2,1)S(1)} collective-permute-done((bf16[80,5120]{1,0:T(8,128)(2,1)S(1)}, bf16[80,5120]{1,0:T(8,128)(2,1)S(1)}, u32[]{:S(2)}, u32[]{:S(2)}) %collective-permute-start.6) | collective-permute-done | bytes 819232 | tf_op jit(solution)/shard_map/ppermute | solution.py:14
  82.7 1.0 constant_dynamic-update-slice_fusion
  83.7 30.2 %all-gather.5.cloned.1.call-done = bf16[5120,896]{1,0:T(8,128)(2,1)} async-done(((bf16[160,896]{1,0:T(8,128)(2,1)}), bf16[5120,896]{1,0:T(8,128)(2,1)}) %all-gather.5.cloned.1.call-update) | async-done | bytes 9175056 | tf_op jit(solution)/shard_map/all_gather | solution.py:79
  113.9 12.7 %fusion.30 = f32[640,896]{1,0:T(8,128)} fusion(bf16[640,5120]{1,0:T(8,128)(2,1)} %constant_dynamic-update-slice_fusion, bf16[5120,896]{1,0:T(8,128)(2,1)} %all-gather.5.cloned.1.call-done), kind=kOutput, calls=%fused_computation.58 | convolution fusion | flops 5872025600 | bytes 18022400 | tf_op jit(solution)/shard_map/dot_general | solution.py:77
  126.6 89.2 %all-gather.7.cloned.1.call-done = bf16[896,5120]{0,1:T(8,128)(2,1)} async-done(((bf16[896,160]{0,1:T(8,128)(2,1)}), bf16[896,5120]{0,1:T(8,128)(2,1)}) %all-gather.7.cloned.1.call-update) | async-done | bytes 9175056 | tf_op jit(solution)/shard_map/all_gather | solution.py:85
  215.8 12.2 %convolution_convert_fusion = bf16[640,5120]{1,0:T(8,128)(2,1)} fusion(bf16[896,5120]{0,1:T(8,128)(2,1)} %all-gather.7.cloned.1.call-done, f32[640,896]{1,0:T(8,128)} %fusion.30), kind=kOutput, calls=%fused_computation.2 | convolution fusion | flops 5880463360 | bytes 18022400 | tf_op jit(solution)/shard_map/dot_general | solution.py:83
  227.9 0.0 reduce-scatter.2.cloned.1.call-update
  228.6 44.7 %reduce-scatter.2.cloned.1.call-done = bf16[80,5120]{1,0:T(8,128)(2,1)} async-done(((bf16[640,5120]{1,0:T(8,128)(2,1)}), bf16[80,5120]{1,0:T(8,128)(2,1)}) %reduce-scatter.2.cloned.1.call-update) | async-done | bytes 819216 | tf_op jit(solution)/shard_map/reduce_scatter | solution.py:88
  273.4 1.6 fusion.16
  275.0 0.4 multiply_reduce_fusion
  275.4 0.5 fusion.13
  276.0 50.2 %all-gather.1 = f32[32,80,64]{1,2,0:T(8,128)S(1)} all-gather(f32[1,80,64]{1,2,0:T(8,128)S(1)} %fusion.19), channel_id=2, replica_groups=mesh['tm'=32,'tensor'=8] {'tm'}, dimensions={0}, use_global_device_ids=true | all-gather | bytes 675840 | tf_op jit(solution)/shard_map/all_gather | solution.py:26
  326.3 3.4 %while.10 = (s32[]{:T(128)}, f32[80,64]{1,0:T(8,128)S(1)}, s32[]{:T(128)}, f32[32,80,64]{1,2,0:T(8,128)S(1)}, s32[]{:T(128)}, /*index=5*/s32[]{:T(128)}, s32[]{:T(128)}) while((s32[]{:T(128)}, f32[80,64]{1,0:T(8,128)S(1)}, s32[]{:T(128)}, f32[32,80,64]{1,2,0:T(8,128)S(1)}, s32[]{:T(128)}, /*index=5*/s32[]{:T(128)}, s32[]{:T(128)}) %tuple.29), condition=%wide.region_6.7_spmd, body=%wide.region_5.6_spmd.sunk | while | flops 5125 | bytes 143475 | solution.py:32
  326.3 0.1 copy.20
  326.4 0.1 copy.20
  326.6 0.1 copy.20
  326.7 0.1 copy.20
  326.9 0.1 copy.20
  327.0 0.1 copy.20
  327.2 0.1 copy.20
  327.3 0.1 copy.20
  327.4 0.1 copy.20
  327.6 0.1 copy.20
  327.7 0.1 copy.20
  327.9 0.1 copy.20
  328.0 0.1 copy.20
  328.1 0.1 copy.20
  328.3 0.1 copy.20
  328.4 0.1 copy.20
  328.6 0.1 copy.20
  328.7 0.1 copy.20
  328.8 0.1 copy.20
  329.0 0.1 copy.20
  329.1 0.1 copy.20
  329.3 0.1 copy.20
  329.4 0.1 copy.20
  329.6 0.1 copy.20
  329.7 0.1 copy.14
  329.7 0.6 add_bitcast_fusion
  (74 shorter events, 0.6 us)
Async XLA Ops:
  7.2 2.3 copy-start
  7.2 106.7 %all-gather.5.cloned.1.call-start = ((), (), s32[]{:S(2)}) async-start(), calls=%async_computation.1 | async-start | bytes 9461760 | tf_op jit(solution)/shard_map/all_gather | solution.py:79
  7.9 207.9 %all-gather.7.cloned.1.call-start = ((), (), s32[]{:S(2)}) async-start(), calls=%async_computation.2 | async-start | bytes 9461760 | tf_op jit(solution)/shard_map/all_gather | solution.py:85
  8.7 264.7 %reduce-scatter.2.cloned.1.call-start = ((), (), s32[]{:S(2)}) async-start(), calls=%async_computation.3 | async-start | bytes 7372800 | tf_op jit(solution)/shard_map/reduce_scatter | solution.py:88
  30.3 13.3 %collective-permute-start = (bf16[80,5120]{1,0:T(8,128)(2,1)}, bf16[80,5120]{1,0:T(8,128)(2,1)}, u32[]{:S(2)}, u32[]{:S(2)}) collective-permute-start(bf16[80,5120]{1,0:T(8,128)(2,1)} %get-tuple-element.43), channel_id=1, source_target_pairs={{0,1},{1,2},{2,3},{3,4},{4,5},{5,6},{6,7},{7,0},{8,9},{9,10},{10,1... | collective-permute-start | bytes 2457608 | tf_op jit(solution)/shard_map/ppermute | solution.py:14
  30.6 13.0 %collective-permute-start.1 = (bf16[80,5120]{1,0:T(8,128)(2,1)}, bf16[80,5120]{1,0:T(8,128)(2,1)S(1)}, u32[]{:S(2)}, u32[]{:S(2)}) collective-permute-start(bf16[80,5120]{1,0:T(8,128)(2,1)} %get-tuple-element.43), channel_id=1, source_target_pairs={{0,7},{1,0},{2,1},{3,2},{4,3},{5,4},{6,5},{7,6},{8,15},{9,8},{10,9... | collective-permute-start | bytes 2457608 | tf_op jit(solution)/shard_map/ppermute | solution.py:17
  43.6 13.2 %collective-permute-start.2 = (bf16[80,5120]{1,0:T(8,128)(2,1)}, bf16[80,5120]{1,0:T(8,128)(2,1)S(1)}, u32[]{:S(2)}, u32[]{:S(2)}) collective-permute-start(bf16[80,5120]{1,0:T(8,128)(2,1)} %collective-permute-done), channel_id=1, source_target_pairs={{0,1},{1,2},{2,3},{3,4},{4,5},{5,6},{6,7},{7,0},{8,9},{9,10},{10,1... | collective-permute-start | bytes 2457608 | tf_op jit(solution)/shard_map/ppermute | solution.py:14
  43.6 13.2 %collective-permute-start.3 = (bf16[80,5120]{1,0:T(8,128)(2,1)S(1)}, bf16[80,5120]{1,0:T(8,128)(2,1)S(1)}, u32[]{:S(2)}, u32[]{:S(2)}) collective-permute-start(bf16[80,5120]{1,0:T(8,128)(2,1)S(1)} %collective-permute-done.1), channel_id=1, source_target_pairs={{0,7},{1,0},{2,1},{3,2},{4,3},{5,4},{6,5},{7,6},{8,15},{9,8},{10,9... | collective-permute-start | bytes 2457608 | tf_op jit(solution)/shard_map/ppermute | solution.py:17
  56.8 13.0 %collective-permute-start.4 = (bf16[80,5120]{1,0:T(8,128)(2,1)S(1)}, bf16[80,5120]{1,0:T(8,128)(2,1)S(1)}, u32[]{:S(2)}, u32[]{:S(2)}) collective-permute-start(bf16[80,5120]{1,0:T(8,128)(2,1)S(1)} %collective-permute-done.2), channel_id=1, source_target_pairs={{0,1},{1,2},{2,3},{3,4},{4,5},{5,6},{6,7},{7,0},{8,9},{9,10},{10,1... | collective-permute-start | bytes 2457608 | tf_op jit(solution)/shard_map/ppermute | solution.py:14
  56.8 13.9 %collective-permute-start.5 = (bf16[80,5120]{1,0:T(8,128)(2,1)S(1)}, bf16[80,5120]{1,0:T(8,128)(2,1)S(1)}, u32[]{:S(2)}, u32[]{:S(2)}) collective-permute-start(bf16[80,5120]{1,0:T(8,128)(2,1)S(1)} %collective-permute-done.3), channel_id=1, source_target_pairs={{0,7},{1,0},{2,1},{3,2},{4,3},{5,4},{6,5},{7,6},{8,15},{9,8},{10,9... | collective-permute-start | bytes 2457608 | tf_op jit(solution)/shard_map/ppermute | solution.py:17
  69.8 13.0 %collective-permute-start.6 = (bf16[80,5120]{1,0:T(8,128)(2,1)S(1)}, bf16[80,5120]{1,0:T(8,128)(2,1)S(1)}, u32[]{:S(2)}, u32[]{:S(2)}) collective-permute-start(bf16[80,5120]{1,0:T(8,128)(2,1)S(1)} %collective-permute-done.4), channel_id=1, source_target_pairs={{0,1},{1,2},{2,3},{3,4},{4,5},{5,6},{6,7},{7,0},{8,9},{9,10},{10,1... | collective-permute-start | bytes 2457608 | tf_op jit(solution)/shard_map/ppermute | solution.py:14
  273.4 1.6 copy-start.1
  273.4 2.1 copy-start.2
  275.0 1.0 copy-start.3
  276.0 54.4 %copy-start.4 = (f32[80,64]{0,1:T(8,128)}, f32[80,64]{0,1:T(8,128)S(1)}, u32[]{:S(2)}) copy-start(f32[80,64]{0,1:T(8,128)S(1)} %fusion.13) | copy-start | bytes 61444
Sparse Core Ops, SparseCore 0:
  10.6 103.2 all-gather.4
  116.5 99.2 all-gather.6
  228.1 45.2 reduce-scatter.1
